TPU v7x, 256 devices: a whole 4x4x8 slice. The times are simulated.
256 devices in a mesh: kv: 8 (over x, core), seq: 8 (over z), vocab: 4 (over y).
Axes of the slice: x: 4, y: 4, z: 8, core: 2. Of those that a mesh axis runs over, the one named last changes fastest.
Arguments:
- hidden_state: bfloat16 [48, 4, 3584], P('kv', 'vocab', 'seq'), may hold values from -6 to 6
- input_projection: bfloat16 [3584, 8, 1024], P('seq', 'kv'), may hold values from -0.09375 to 0.09375
- output_projection: bfloat16 [8, 512, 3584], P('kv', None, 'seq'), may hold values from -0.09375 to 0.09375
- norm_pre_attention: float32 [3584], P('seq'), may hold values from 0.1 to 1.9
- norm_post_attention: float32 [3584], P('seq'), may hold values from 0.1 to 1.9
- norm_pre_feedforward: float32 [3584], P('seq'), may hold values from 0.1 to 1.9
- norm_post_feedforward: float32 [3584], P('seq'), may hold values from 0.1 to 1.9
- norm_final: float32 [3584], P('seq'), may hold values from 0.1 to 1.9
- cache_keys: bfloat16 [4, 16384, 8, 256], P('vocab', 'seq', 'kv')
- cache_values: bfloat16 [4, 16384, 8, 256], P('vocab', 'seq', 'kv')
- cache_length: int32 [4], P('vocab'), may hold values from 1 to 16379, as said below
- ancestors: int32 [4, 48, 48], P('vocab'), may hold values from 0 to 1, as said below
- accepted_path: int32 [4, 5], P('vocab'), may hold values from 0 to 47, as said below
- gate_up_weight: bfloat16 [3584, 2, 14336], P('seq', None, ('kv', 'vocab')), may hold values from -0.09375 to 0.09375
- down_weight: bfloat16 [14336, 3584], P(('kv', 'vocab'), 'seq'), may hold values from -0.046875 to 0.046875
- draft_weight: bfloat16 [4, 3584, 3584], P(None, 'seq', ('kv', 'vocab')), may hold values from -0.09375 to 0.09375
- draft_bias: float32 [4, 3584], P(None, ('kv', 'vocab')), may hold values from -3 to 3
- vocab_weight: bfloat16 [131072, 3584], P(('kv', 'seq', 'vocab'))
- candidate_tokens: int32 [5, 48, 4, 8], replicated, may hold values from 0 to 131071
Outputs:
- keys_updated: bfloat16 [4, 16384, 8, 256], P('vocab', 'seq', 'kv')
- values_updated: bfloat16 [4, 16384, 8, 256], P('vocab', 'seq', 'kv')
- log_normalizer: float32 [5, 48, 4], replicated
- candidate_logits: float32 [5, 48, 4, 8], replicated
Inputs may be any that keep to these rules, and one draw needn't show every extreme that they name: The first cache_length[k] slots of tenant k's cache are filled; in every draw some tenant holds exactly 16379. ancestors[k, t, u] is 1 exactly when u is t or an ancestor of t in tenant k's tree; node 0 is the root and every parent has a lower index than its child. accepted_path[k] lists 5 nodes of tenant k's tree from the root down, each the parent of the next; the last of them is node 47.
All inputs are finite; a program needn't handle non-finite values.
Results may differ from a plain program's by a relative error of at most 0.02.
Values may be sent and summed in bfloat16 or wider, within the bound.
A program may use at most 64 MiB of HBM per device.

v0:
```python
import jax
import jax.numpy as jnp
from jax import lax
from jax.sharding import PartitionSpec as P

MODEL_WIDTH = 3584
HEAD_SIZE = 256
CAND = 8
EPSILON = 1e-06
SCORE_CAP = 50.0
LOGIT_CAP = 30.0


def apply_rotary(vectors, token_positions):
    half_dim = vectors.shape[-1] // 2
    frequency = 10000.0 ** (-2.0 * jnp.arange(half_dim, dtype=jnp.float32) / vectors.shape[-1])
    angles = token_positions.astype(jnp.float32)[..., None] * frequency
    cosine = jnp.cos(angles)
    sine_part = jnp.sin(angles)
    first_half = vectors[..., :half_dim]
    second_half = vectors[..., half_dim:]
    return jnp.concatenate(
        [
            first_half * cosine - second_half * sine_part,
            second_half * cosine + first_half * sine_part,
        ],
        axis=-1,
    )


def capped_weight(scores):
    return jnp.exp(SCORE_CAP * jnp.tanh(scores * 0.0625 / SCORE_CAP))


def row_inverse(values):
    totals = lax.psum(jnp.sum(values * values, axis=-1), "seq")
    return lax.rsqrt(totals / MODEL_WIDTH + EPSILON)[:, None]


def gated_units(gate_up, squares):
    inverse = lax.rsqrt(squares / MODEL_WIDTH + EPSILON)[:, None]
    return (
        jax.nn.gelu(gate_up[:, 0] * inverse, approximate=True) * (gate_up[:, 1] * inverse)
    ).astype(jnp.bfloat16)


def local(
    hidden_state,
    input_projection,
    output_projection,
    norm_pre_attention,
    norm_post_attention,
    norm_pre_feedforward,
    norm_post_feedforward,
    norm_final,
    cache_keys,
    cache_values,
    cache_length,
    ancestors,
    accepted_path,
    gate_up_weight,
    down_weight,
    draft_weight,
    draft_bias,
    vocab_weight,
    candidate_tokens,
):
    tok_block = hidden_state.shape[0]
    kv_count = lax.axis_size("kv")
    tenants = lax.axis_size("vocab")
    tree_size = tok_block * kv_count
    own_state = hidden_state[:, 0, :]
    tenant_state = lax.all_gather(own_state, "kv", axis=0, tiled=True)
    tenant_float = tenant_state.astype(jnp.float32)
    scaled_input = (tenant_float * norm_pre_attention).astype(jnp.bfloat16)
    projected_rows = jnp.einsum(
        "td,dhc->thc", scaled_input, input_projection, preferred_element_type=jnp.float32
    )
    projected_rows, squares = lax.psum(
        (projected_rows, jnp.sum(tenant_float * tenant_float, axis=-1)), "seq"
    )
    projected_rows = projected_rows * lax.rsqrt(squares / MODEL_WIDTH + EPSILON)[:, None, None]
    head_count = projected_rows.shape[1]
    depths = jnp.sum(ancestors[0], axis=-1) - 1
    length = cache_length[0]
    token_positions = length + depths
    query_rows = apply_rotary(
        projected_rows[:, :, : 2 * HEAD_SIZE].reshape(tree_size, head_count, 2, HEAD_SIZE),
        token_positions[:, None, None],
    ).astype(jnp.bfloat16)
    new_keys = apply_rotary(
        projected_rows[:, :, 2 * HEAD_SIZE : 3 * HEAD_SIZE], token_positions[:, None]
    ).astype(jnp.bfloat16)
    new_values = projected_rows[:, :, 3 * HEAD_SIZE :].astype(jnp.bfloat16)
    block_size = cache_keys.shape[1]
    block_start = lax.axis_index("seq") * block_size
    cache_cells = block_start + jnp.arange(block_size, dtype=jnp.int32)
    scores = jnp.einsum(
        "thgc,shc->thgs", query_rows, cache_keys[0], preferred_element_type=jnp.float32
    )
    weights = jnp.where((cache_cells < length)[None, None, None, :], capped_weight(scores), 0.0)
    numerator = jnp.einsum(
        "thgs,shc->thgc",
        weights.astype(jnp.bfloat16),
        cache_values[0],
        preferred_element_type=jnp.float32,
    )
    numerator, denominator = lax.psum((numerator, jnp.sum(weights, axis=-1)), "seq")
    tree_scores = jnp.einsum(
        "thgc,uhc->thgu", query_rows, new_keys, preferred_element_type=jnp.float32
    )
    tree_weights = jnp.where(ancestors[0][:, None, None, :] > 0, capped_weight(tree_scores), 0.0)
    numerator = numerator + jnp.einsum(
        "thgu,uhc->thgc",
        tree_weights.astype(jnp.bfloat16),
        new_values,
        preferred_element_type=jnp.float32,
    )
    denominator = denominator + jnp.sum(tree_weights, axis=-1)
    attended = (
        (numerator / denominator[..., None])
        .astype(jnp.bfloat16)
        .reshape(tree_size, head_count * 2 * HEAD_SIZE)
    )
    out_matrix = output_projection.reshape(head_count * 2 * HEAD_SIZE, output_projection.shape[2])
    attention_out = lax.psum_scatter(
        jnp.dot(attended, out_matrix, preferred_element_type=jnp.float32),
        "kv",
        scatter_dimension=0,
        tiled=True,
    )
    first_sum = (
        own_state.astype(jnp.float32)
        + attention_out * row_inverse(attention_out) * norm_post_attention
    ).astype(jnp.bfloat16)
    all_state = lax.all_gather(first_sum, ("kv", "vocab"), axis=0, tiled=True)
    all_float = all_state.astype(jnp.float32)
    scaled_ffn = (all_float * norm_pre_feedforward).astype(jnp.bfloat16)
    gate_up = jnp.einsum(
        "td,dcf->tcf", scaled_ffn, gate_up_weight, preferred_element_type=jnp.float32
    )
    ffn_squares = jnp.sum(all_float * all_float, axis=-1)
    gate_up, ffn_squares = lax.psum((gate_up, ffn_squares), "seq")
    activated = gated_units(gate_up, ffn_squares)
    ffn_out = lax.psum_scatter(
        jnp.dot(activated, down_weight, preferred_element_type=jnp.float32),
        ("kv", "vocab"),
        scatter_dimension=0,
        tiled=True,
    )
    first_float = first_sum.astype(jnp.float32)
    second_sum = (first_float + ffn_out * row_inverse(ffn_out) * norm_post_feedforward).astype(
        jnp.bfloat16
    )
    second_float = second_sum.astype(jnp.float32)
    normed = (second_float * row_inverse(second_float) * norm_final).astype(jnp.bfloat16)
    gathered = lax.all_gather(normed, ("kv", "vocab"), axis=0, tiled=True)
    lifted = jnp.einsum("td,ndc->tnc", gathered, draft_weight, preferred_element_type=jnp.float32)
    lifted = lax.psum(lifted.astype(jnp.bfloat16), "seq").astype(jnp.float32)
    branch = jax.nn.silu(lifted + draft_bias).astype(jnp.bfloat16)
    row_count = gathered.shape[0]
    vocab_rows = vocab_weight.shape[0]
    draft_count = branch.shape[1]
    columns = vocab_weight
    base_logits = lax.dot_general(
        lax.all_gather(gathered, "seq", axis=1, tiled=True),
        columns,
        (((1,), (1,)), ((), ())),
        preferred_element_type=jnp.float32,
    )
    columns = vocab_weight
    draft_extra = jnp.einsum(
        "tnc,vc->tnv",
        lax.all_gather(branch, ("kv", "vocab"), axis=2, tiled=True),
        columns,
        preferred_element_type=jnp.float32,
    )
    raw_logits = jnp.concatenate(
        [base_logits[:, None, :], base_logits[:, None, :] + draft_extra], axis=1
    )
    logits = LOGIT_CAP * jnp.tanh(raw_logits / LOGIT_CAP)
    totals = jnp.sum(jnp.exp(logits), axis=-1)
    head_total = draft_count + 1
    candidates = candidate_tokens.reshape(head_total, kv_count, tok_block, tenants, CAND)
    candidates = jnp.transpose(candidates, (0, 1, 3, 2, 4)).reshape(head_total, row_count, CAND)
    candidates = jnp.transpose(candidates, (1, 0, 2))
    vocab_start = lax.axis_index(("kv", "seq", "vocab")) * vocab_rows
    local_tokens = candidates - vocab_start
    entry_index = jnp.arange(vocab_rows, dtype=jnp.int32)
    picked = jnp.stack(
        [
            jnp.sum(
                jnp.where(entry_index == local_tokens[:, :, column : column + 1], logits, 0.0),
                axis=-1,
            )
            for column in range(CAND)
        ],
        axis=-1,
    )
    totals, picked = lax.psum((totals, picked), ("kv", "seq", "vocab"))
    log_totals = jnp.transpose(jnp.log(totals)).reshape(head_total, kv_count, tenants, tok_block)
    log_normalizer = jnp.transpose(log_totals, (0, 1, 3, 2)).reshape(head_total, tree_size, tenants)
    picked = jnp.transpose(picked, (1, 0, 2)).reshape(
        head_total, kv_count, tenants, tok_block, CAND
    )
    candidate_logits = jnp.transpose(picked, (0, 1, 3, 2, 4)).reshape(
        head_total, tree_size, tenants, CAND
    )
    accept_count = accepted_path.shape[1]
    slot_rows = length + jnp.arange(accept_count, dtype=jnp.int32)
    tree_nodes = jnp.arange(tree_size, dtype=jnp.int32)
    matches = (cache_cells[:, None, None] == slot_rows[None, :, None]) & (
        accepted_path[0][None, :, None] == tree_nodes[None, None, :]
    )
    selector = jnp.sum(matches.astype(jnp.float32), axis=1)
    written = jnp.sum(selector, axis=-1) > 0.0
    selector = selector.astype(jnp.bfloat16)

    def write_path(old_block, fresh_rows):
        moved_rows = jnp.dot(
            selector, fresh_rows.reshape(tree_size, -1), preferred_element_type=jnp.float32
        ).astype(jnp.bfloat16)
        return jnp.where(
            written[:, None], moved_rows, old_block[0].reshape(block_size, -1)
        ).reshape(old_block.shape)

    keys_updated = write_path(cache_keys, new_keys)
    values_updated = write_path(cache_values, new_values)
    return (keys_updated, values_updated, log_normalizer, candidate_logits)


def solution(mesh):
    placed = (
        P("kv", "vocab", "seq"),
        P("seq", "kv", None),
        P("kv", None, "seq"),
        P("seq"),
        P("seq"),
        P("seq"),
        P("seq"),
        P("seq"),
        P("vocab", "seq", "kv", None),
        P("vocab", "seq", "kv", None),
        P("vocab"),
        P("vocab", None, None),
        P("vocab", None),
        P("seq", None, ("kv", "vocab")),
        P(("kv", "vocab"), "seq"),
        P(None, "seq", ("kv", "vocab")),
        P(None, ("kv", "vocab")),
        P(("kv", "seq", "vocab"), None),
        P(),
    )
    return jax.shard_map(
        local,
        mesh=mesh,
        in_specs=placed,
        out_specs=(P("vocab", "seq", "kv", None), P("vocab", "seq", "kv", None), P(), P()),
        check_vma=False,
    )
```

profile of v0, /device:TPU:1, one launch (start us, length us, event | category | flops | bytes accessed | tf_op | source)
XLA Modules:
  0.0 775.7 jit_solution(17245792410160348582)
XLA Ops:
  7.2 0.8 copy.52
  8.1 15.8 %all-gather = bf16[48,1,448]{2,1,0:T(2,128)(2,1)S(1)} all-gather(bf16[6,1,448]{2,1,0:T(2,128)(2,1)S(1)} %copy.52), channel_id=2, replica_groups=mesh['kv'=8,'seq'=8,'vocab'=4] {'kv'}, dimensions={0}, use_global_device_ids=true | all-gather | bytes 48384 | tf_op jit(solution)/shard_map/all_gather | solution.py:73
  24.0 2.2 convolution_bitcast_fusion
  26.3 15.0 %psum.85 = f32[48]{0:T(128)S(1)} all-reduce(f32[48]{0:T(128)S(1)} %fusion.56), channel_id=1, replica_groups=mesh['kv'=8,'seq'=8,'vocab'=4] {'seq'}, use_global_device_ids=true, to_apply=%region_4.5 | all-reduce | flops 48 | bytes 384 | tf_op jit(solution)/shard_map/psum | solution.py:79
  42.0 0.7 compare_bitcast_fusion
  42.7 0.8 reduce_sum.178
  43.9 50.6 %all-reduce.10.cloned.1.call-done = f32[48,1,1024]{2,0,1:T(8,128)} async-done(((f32[48,1,1024]{2,0,1:T(8,128)}), f32[48,1,1024]{2,0,1:T(8,128)}) %all-reduce.10.cloned.1.call-update) | async-done | bytes 196624 | tf_op jit(solution)/shard_map/psum | solution.py:79
  94.5 1.0 broadcast_multiply_fusion
  95.8 1.2 fusion.93
  97.1 12.7 %psum.87 = f32[48,1,2]{0,2,1:T(2,128)S(1)} all-reduce(f32[48,1,2]{0,2,1:T(2,128)S(1)} %bitcast.224), channel_id=1, replica_groups=mesh['kv'=8,'seq'=8,'vocab'=4] {'seq'}, use_global_device_ids=true, to_apply=%region_8.9 | all-reduce | flops 96 | bytes 768 | tf_op jit(solution)/shard_map/psum | solution.py:108
  109.8 2.0 convolution_bitcast_fusion.1
  112.0 73.8 %all-reduce.12.cloned.1.call-done = f32[48,1,2,256]{3,0,2,1:T(8,128)} async-done(((f32[48,1,2,256]{3,0,2,1:T(8,128)}), f32[48,1,2,256]{3,0,2,1:T(8,128)}) %all-reduce.12.cloned.1.call-update) | async-done | bytes 98320 | tf_op jit(solution)/shard_map/psum | solution.py:108
  185.8 1.1 fusion.24
  187.0 0.2 fusion.35
  187.3 18.1 %fusion = f32[8,448]{1,0:T(8,128)S(1)} fusion(f32[48,448]{1,0:T(8,128)S(1)} %fusion.35), kind=kCustom, calls=%all-reduce-scatter | all-reduce-scatter fusion | flops 28673 | bytes 101376
  205.3 3.4 collective-permute-start
  208.8 1.6 collective-permute-start.1
  210.4 0.6 dynamic-slice.6
  212.0 11.6 %psum.88 = f32[6]{0:T(128)S(1)} all-reduce(f32[6]{0:T(128)S(1)} %multiply_reduce_fusion.2), channel_id=1, replica_groups=mesh['kv'=8,'seq'=8,'vocab'=4] {'seq'}, use_global_device_ids=true, to_apply=%region_12.13 | all-reduce | flops 6 | bytes 48 | tf_op jit(solution)/shard_map/psum | solution.py:36
  223.7 45.5 %all-gather.1 = bf16[32,6,448]{2,1,0:T(8,128)(2,1)S(1)} all-gather(bf16[1,6,448]{2,1,0:T(8,128)(2,1)S(1)} %bitcast.223), channel_id=1, replica_groups=mesh['kv'=8,'seq'=8,'vocab'=4] {'kv','vocab'}, dimensions={0}, use_global_device_ids=true | all-gather | bytes 177408 | tf_op jit(solution)/shard_map/all_gather | solution.py:136
  269.4 1.3 fusion.33
  270.8 11.5 %psum.90 = f32[192]{0:T(256)S(1)} all-reduce(f32[192]{0:T(256)S(1)} %multiply_reduce_fusion), channel_id=1, replica_groups=mesh['kv'=8,'seq'=8,'vocab'=4] {'seq'}, use_global_device_ids=true, to_apply=%region_15.16 | all-reduce | flops 192 | bytes 1536 | tf_op jit(solution)/shard_map/psum | solution.py:143
  282.3 57.1 %all-reduce.14.cloned.1.call-done = f32[192,2,448]{2,0,1:T(8,128)} async-done(((f32[192,2,448]{2,0,1:T(8,128)}), f32[192,2,448]{2,0,1:T(8,128)}) %all-reduce.14.cloned.1.call-update) | async-done | bytes 688144 | tf_op jit(solution)/shard_map/psum | solution.py:143
  339.4 1.6 fusion.53
  341.1 68.1 %fusion.1 = f32[8,448]{1,0:T(8,128)S(1)} fusion(f32[192,448]{1,0:T(8,128)S(1)} %fusion.53), kind=kCustom, calls=%all-reduce-scatter.1 | all-reduce-scatter fusion | flops 114689 | bytes 359424
  409.1 1.9 collective-permute-start.2
  411.1 1.9 collective-permute-start.3
  413.0 1.4 collective-permute-start.9
  414.4 1.9 collective-permute-start.4
  416.4 1.9 collective-permute-start.5
  418.3 5.9 collective-permute-start.6
  424.2 6.8 collective-permute-start.7
  431.0 3.9 collective-permute-start.8
  435.0 0.6 dynamic-slice.10
  436.3 0.8 concatenate.35
  437.2 12.6 %psum.91 = f32[6]{0:T(128)S(1)} all-reduce(f32[6]{0:T(128)S(1)} %multiply_reduce_fusion.1), channel_id=1, replica_groups=mesh['kv'=8,'seq'=8,'vocab'=4] {'seq'}, use_global_device_ids=true, to_apply=%region_18.19 | all-reduce | flops 6 | bytes 48 | tf_op jit(solution)/shard_map/psum | solution.py:36
  450.0 10.7 %psum.92 = f32[6]{0:T(128)S(1)} all-reduce(f32[6]{0:T(128)S(1)} %get-tuple-element.17), channel_id=1, replica_groups=mesh['kv'=8,'seq'=8,'vocab'=4] {'seq'}, use_global_device_ids=true, to_apply=%region_20.21 | all-reduce | flops 6 | bytes 48 | tf_op jit(solution)/shard_map/psum | solution.py:36
  460.8 48.2 %all-gather.2 = bf16[32,6,448]{2,1,0:T(8,128)(2,1)S(1)} all-gather(bf16[1,6,448]{2,1,0:T(8,128)(2,1)S(1)} %fusion.82), channel_id=1, replica_groups=mesh['kv'=8,'seq'=8,'vocab'=4] {'kv','vocab'}, dimensions={0}, use_global_device_ids=true | all-gather | bytes 177408 | tf_op jit(solution)/shard_map/all_gather | solution.py:157
  509.1 0.9 convolution_convert_fusion.2
  510.2 0.8 reshape.410
  511.0 0.2 all-gather.7.cloned.1.call-start
  511.2 64.1 %all-reduce.16.cloned.1.call-done = bf16[192,4,112]{2,0,1:T(8,128)(2,1)} async-done(((bf16[192,4,112]{2,0,1:T(8,128)(2,1)}), bf16[192,4,112]{2,0,1:T(8,128)(2,1)}) %all-reduce.16.cloned.1.call-update) | async-done | bytes 172048 | tf_op jit(solution)/shard_map/psum | solution.py:159
  575.3 1.0 multiply_convert_fusion
  576.3 0.9 copy.60
  577.5 0.4 copy.63
  577.9 0.6 sub.35
  578.7 0.3 convert_reduce_fusion
  579.1 0.6 copy_bitcast_fusion
  579.7 0.6 copy_bitcast_fusion.2
  580.3 0.6 copy_bitcast_fusion.4
  580.9 0.6 copy_bitcast_fusion.6
  581.5 2.5 fusion.6
  584.1 1.5 fusion.8
  585.5 30.5 %all-gather.9.cloned.1.call-done = bf16[8,448,192]{1,2,0:T(8,128)(2,1)} async-done(((bf16[1,448,192]{1,2,0:T(8,128)(2,1)}), bf16[8,448,192]{1,2,0:T(8,128)(2,1)}) %all-gather.9.cloned.1.call-update) | async-done | bytes 1376272 | tf_op jit(solution)/shard_map/all_gather | solution.py:166
  616.1 2.3 copy.59
  618.4 2.7 reshape.412
  621.1 3.8 fusion.95
  625.0 52.4 %all-gather.7.cloned.1.call-done = bf16[192,4,3584]{0,1,2:T(4,128)(2,1)} async-done(((bf16[192,4,112]{0,1,2:T(4,128)(2,1)}), bf16[192,4,3584]{0,1,2:T(4,128)(2,1)}) %all-gather.7.cloned.1.call-update) | async-done | bytes 5505040 | tf_op jit(solution)/shard_map/all_gather | solution.py:174
  677.3 8.2 %fusion.17 = f32[192,4,512]{2,0,1:T(8,128)S(1)} fusion(bf16[512,3584]{1,0:T(8,128)(2,1)} %param.36, bf16[192,4,3584]{0,1,2:T(4,128)(2,1)} %all-gather.7.cloned.1.call-done, f32[192,512]{1,0:T(8,128)S(1)} %fusion.95), kind=kOutput, calls=%fused_computation.38 | convolution fusion | flops 2818965504 | bytes 11141120 | tf_op jit(solution)/shard_map/tnc,vc->tnv/dot_general | solution.py:172
  685.6 4.4 select_reduce_fusion
  690.2 0.8 reshape.400
  691.2 0.2 reshape.401
  691.4 76.6 %all-reduce.4 = (f32[192,5]{0,1:T(8,128)S(1)}, f32[5,48,4,8]{1,3,2,0:T(8,128)}) all-reduce(f32[192,5]{0,1:T(8,128)S(1)} %get-tuple-element.19, f32[5,48,4,8]{1,3,2,0:T(8,128)S(1)} %reshape.401), channel_id=1, replica_groups=mesh['kv'=8,'seq'=8,'vocab'=4] {'kv','seq','vocab'}, use_global_device_ids=true, to_apply=%region_23.24 | all-reduce | flops 8640 | bytes 69120 | tf_op jit(solution)/shard_map/psum | solution.py:200
  768.1 0.7 reshape.399
  (118 shorter events, 3.5 us)
Async XLA Ops:
  7.2 262.2 %copy-start = (bf16[448,2,448]{2,1,0:T(2,128)(2,1)S(1)}, bf16[448,2,448]{2,1,0:T(2,128)(2,1)}, u32[]{:S(2)}) copy-start(bf16[448,2,448]{2,1,0:T(2,128)(2,1)} %param.32) | copy-start | bytes 2408452
  7.2 88.7 %copy-start.2 = (bf16[1,2048,1,256]{3,1,2,0:T(8,128)(2,1)S(1)}, bf16[1,2048,1,256]{3,1,2,0:T(8,128)(2,1)}, u32[]{:S(2)}) copy-start(bf16[1,2048,1,256]{3,1,2,0:T(8,128)(2,1)} %param.27) | copy-start | bytes 3145732
  7.2 87.3 %all-reduce.10.cloned.1.call-start = ((), (), s32[]{:S(2)}) async-start(), calls=%async_computation | async-start | bytes 393216 | tf_op jit(solution)/shard_map/psum | solution.py:79
  26.1 83.6 %copy-start.1 = (bf16[1,2048,1,256]{3,1,2,0:T(8,128)(2,1)S(1)}, bf16[1,2048,1,256]{3,1,2,0:T(8,128)(2,1)}, u32[]{:S(2)}) copy-start(bf16[1,2048,1,256]{3,1,2,0:T(8,128)(2,1)} %param.28) | copy-start | bytes 3145732
  26.2 159.7 %all-reduce.12.cloned.1.call-start = ((), (), s32[]{:S(2)}) async-start(), calls=%async_computation.1 | async-start | bytes 196608 | tf_op jit(solution)/shard_map/psum | solution.py:108
  97.1 89.9 %copy-start.3 = (bf16[1,512,448]{1,2,0:T(8,128)(2,1)S(1)}, bf16[1,512,448]{1,2,0:T(8,128)(2,1)}, u32[]{:S(2)}) copy-start(bf16[1,512,448]{1,2,0:T(8,128)(2,1)} %param.21) | copy-start | bytes 1376260
  97.1 113.3 %copy-start.20 = (u32[256]{0:T(256)S(1)}, u32[256]{0:T(256)}, u32[]{:S(2)}) copy-start(u32[256]{0:T(256)} %constant.87) | copy-start | bytes 3076
  97.1 126.5 %copy-start.13 = (bf16[6,1,448]{2,0,1:T(8,128)(2,1)S(1)}, bf16[6,1,448]{2,0,1:T(8,128)(2,1)}, u32[]{:S(2)}) copy-start(bf16[6,1,448]{2,0,1:T(8,128)(2,1)} %param.19) | copy-start | bytes 16132
  97.1 126.5 %copy-start.16 = (f32[448]{0:T(512)S(1)}, f32[448]{0:T(512)}, u32[]{:S(2)}) copy-start(f32[448]{0:T(512)} %param.23) | copy-start | bytes 5380
  109.8 159.6 %copy-start.14 = (f32[448]{0:T(512)S(1)}, f32[448]{0:T(512)}, u32[]{:S(2)}) copy-start(f32[448]{0:T(512)} %param.24) | copy-start | bytes 5380
  111.8 227.7 %all-reduce.14.cloned.1.call-start = ((), (), s32[]{:S(2)}) async-start(), calls=%async_computation.2 | async-start | bytes 1572864 | tf_op jit(solution)/shard_map/psum | solution.py:143
  205.3 6.3 collective-permute-start
  208.8 2.8 collective-permute-start.1
  270.6 164.4 %copy-start.19 = (u32[256]{0:T(256)S(1)}, u32[256]{0:T(256)}, u32[]{:S(2)}) copy-start(u32[256]{0:T(256)} %constant.91) | copy-start | bytes 3076
  270.6 179.2 %copy-start.17 = (f32[448]{0:T(512)S(1)}, f32[448]{0:T(512)}, u32[]{:S(2)}) copy-start(f32[448]{0:T(512)} %param.25) | copy-start | bytes 5380
  270.6 190.1 %copy-start.18 = (f32[448]{0:T(512)S(1)}, f32[448]{0:T(512)}, u32[]{:S(2)}) copy-start(f32[448]{0:T(512)} %param.26) | copy-start | bytes 5380
  270.6 238.5 %copy-start.4 = (bf16[4,448,112]{2,1,0:T(8,128)(2,1)S(1)}, bf16[4,448,112]{2,1,0:T(8,128)(2,1)}, u32[]{:S(2)}) copy-start(bf16[4,448,112]{2,1,0:T(8,128)(2,1)} %param.34) | copy-start | bytes 1204228
  270.7 304.6 %all-reduce.16.cloned.1.call-start = ((), (), s32[]{:S(2)}) async-start(), calls=%async_computation.3 | async-start | bytes 393216 | tf_op jit(solution)/shard_map/psum | solution.py:159
  341.1 234.2 %copy-start.15 = (f32[4,112]{1,0:T(4,128)S(1)}, f32[4,112]{1,0:T(4,128)}, u32[]{:S(2)}) copy-start(f32[4,112]{1,0:T(4,128)} %param.35) | copy-start | bytes 5380
  409.1 15.1 %collective-permute-start.2 = (f32[8,448]{1,0:T(8,128)S(1)}, f32[8,448]{1,0:T(8,128)S(1)}, u32[]{:S(2)}, u32[]{:S(2)}) collective-permute-start(f32[8,448]{1,0:T(8,128)S(1)} %fusion.1), channel_id=1, source_target_pairs={{0,1},{1,2},{2,3},{3,32},{32,33},{33,34},{34,35},{35,64},{64,65},{... | collective-permute-start | bytes 43016
  411.1 20.0 %collective-permute-start.3 = (f32[8,448]{1,0:T(8,128)S(1)}, f32[8,448]{1,0:T(8,128)S(1)}, u32[]{:S(2)}, u32[]{:S(2)}) collective-permute-start(f32[8,448]{1,0:T(8,128)S(1)} %fusion.1), channel_id=1, source_target_pairs={{0,2},{1,3},{2,32},{3,33},{32,34},{33,35},{34,64},{35,65},{64,66},... | collective-permute-start | bytes 43016
  413.0 164.3 %copy-start.5 = (s32[5,48,4,8]{1,3,2,0:T(8,128)S(1)}, s32[5,48,4,8]{1,3,2,0:T(8,128)}, u32[]{:S(2)}) copy-start(s32[5,48,4,8]{1,3,2,0:T(8,128)} %param.37) | copy-start | bytes 92164
  413.0 5.3 collective-permute-start.9
  414.4 21.8 %collective-permute-start.4 = (f32[8,448]{1,0:T(8,128)S(1)}, f32[8,448]{1,0:T(8,128)S(1)}, u32[]{:S(2)}, u32[]{:S(2)}) collective-permute-start(f32[8,448]{1,0:T(8,128)S(1)} %fusion.1), channel_id=1, source_target_pairs={{0,3},{1,32},{2,33},{3,34},{32,35},{33,64},{34,65},{35,66},{64,67}... | collective-permute-start | bytes 43016
  416.4 19.9 %collective-permute-start.5 = (f32[8,448]{1,0:T(8,128)S(1)}, f32[8,448]{1,0:T(8,128)S(1)}, u32[]{:S(2)}, u32[]{:S(2)}) collective-permute-start(f32[8,448]{1,0:T(8,128)S(1)} %fusion.1), channel_id=1, source_target_pairs={{0,32},{1,33},{2,34},{3,35},{32,64},{33,65},{34,66},{35,67},{64,96... | collective-permute-start | bytes 43016
  418.3 17.9 %collective-permute-start.6 = (f32[8,448]{1,0:T(8,128)S(1)}, f32[8,448]{1,0:T(8,128)S(1)}, u32[]{:S(2)}, u32[]{:S(2)}) collective-permute-start(f32[8,448]{1,0:T(8,128)S(1)} %fusion.1), channel_id=1, source_target_pairs={{0,33},{1,34},{2,35},{3,64},{32,65},{33,66},{34,67},{35,96},{64,97... | collective-permute-start | bytes 43016
  424.2 12.1 %collective-permute-start.7 = (f32[8,448]{1,0:T(8,128)S(1)}, f32[8,448]{1,0:T(8,128)S(1)}, u32[]{:S(2)}, u32[]{:S(2)}) collective-permute-start(f32[8,448]{1,0:T(8,128)S(1)} %fusion.1), channel_id=1, source_target_pairs={{0,34},{1,35},{2,64},{3,65},{32,66},{33,67},{34,96},{35,97},{64,98... | collective-permute-start | bytes 43016
  431.0 5.2 collective-permute-start.8
  510.1 106.0 %all-gather.9.cloned.1.call-start = ((), (), s32[]{:S(2)}) async-start(), calls=%async_computation.5 | async-start | bytes 1769472 | tf_op jit(solution)/shard_map/all_gather | solution.py:166
  511.0 67.6 %copy-start.21 = (s32[1,5]{1,0:T(1,128)S(1)}, s32[1,5]{1,0:T(1,128)}, u32[]{:S(2)}) copy-start(s32[1,5]{1,0:T(1,128)} %param.31) | copy-start | bytes 64
  511.0 166.3 %all-gather.7.cloned.1.call-start = ((), (), s32[]{:S(2)}) async-start(), calls=%async_computation.4 | async-start | bytes 7569408 | tf_op jit(solution)/shard_map/all_gather | solution.py:174
  624.9 60.7 %copy-start.6 = (s32[192,5]{0,1:T(8,128)S(1)}, s32[192,5]{0,1:T(8,128)}, u32[]{:S(2)}) copy-start(s32[192,5]{0,1:T(8,128)} %get-tuple-element.43) | copy-start | bytes 11524
  624.9 60.7 %copy-start.7 = (s32[192,5]{0,1:T(8,128)S(1)}, s32[192,5]{0,1:T(8,128)}, u32[]{:S(2)}) copy-start(s32[192,5]{0,1:T(8,128)} %get-tuple-element.44) | copy-start | bytes 11524
  624.9 60.7 %copy-start.8 = (s32[192,5]{0,1:T(8,128)S(1)}, s32[192,5]{0,1:T(8,128)}, u32[]{:S(2)}) copy-start(s32[192,5]{0,1:T(8,128)} %get-tuple-element.45) | copy-start | bytes 11524
  624.9 60.7 %copy-start.9 = (s32[192,5]{0,1:T(8,128)S(1)}, s32[192,5]{0,1:T(8,128)}, u32[]{:S(2)}) copy-start(s32[192,5]{0,1:T(8,128)} %get-tuple-element.46) | copy-start | bytes 11524
  624.9 60.7 %copy-start.10 = (s32[192,5]{0,1:T(8,128)S(1)}, s32[192,5]{0,1:T(8,128)}, u32[]{:S(2)}) copy-start(s32[192,5]{0,1:T(8,128)} %get-tuple-element.47) | copy-start | bytes 11524
  624.9 60.7 %copy-start.11 = (s32[192,5]{0,1:T(8,128)S(1)}, s32[192,5]{0,1:T(8,128)}, u32[]{:S(2)}) copy-start(s32[192,5]{0,1:T(8,128)} %get-tuple-element.48) | copy-start | bytes 11524
  625.0 60.7 %copy-start.12 = (s32[192,5]{0,1:T(8,128)S(1)}, s32[192,5]{0,1:T(8,128)}, u32[]{:S(2)}) copy-start(s32[192,5]{0,1:T(8,128)} %get-tuple-element.49) | copy-start | bytes 11524
Sparse Core Ops, SparseCore 0:
  26.3 68.1 all-reduce.9
  111.9 73.9 all-reduce.11
  270.8 68.6 all-reduce.13
  510.2 65.0 all-reduce.15
  576.9 39.1 all-gather.8
  618.5 58.7 all-gather.6
where the time goes:
time: 777 us; the launch traced here: 776 us
  blocking collectives  346 us (45%)
  waiting for transfers between devices  329 us (42%)
  starting transfers between devices  31.2 us (4%)
  matrix products  26.7 us (3%)
  between operations  16.9 us (2%)
  local copies, waits for them, and re-layouts  16 us (2%)
  other arithmetic  9.93 us (1%)
    unnamed x2, blocking collectives  86.2 us
    psum x1, blocking collectives, local(): totals, picked = lax.psum((totals, picked), ('kv', 'seq', 'vocab'))  76.6 us
    psum x1, waiting for transfers between devices, local(): lax.psum((numerator, jnp.sum(weights, axis=-1)), 'seq')  73.8 us
    psum x1, waiting for transfers between devices, local(): lifted = lax.psum(lifted.astype(jnp.bfloat16), 'seq').astype(jnp.float32)  64.1 us
    psum x1, waiting for transfers between devices, local(): gate_up, ffn_squares = lax.psum((gate_up, ffn_squares), 'seq')  57.1 us
    all_gather x1, waiting for transfers between devices, local(): lax.all_gather(branch, ('kv', 'vocab'), axis=2, tiled=True)  52.4 us
    psum x1, waiting for transfers between devices, local(): lax.psum((projected_rows, jnp.sum(tenant_float * tenant_float, axis=-1)),...  50.6 us
    all_gather x1, blocking collectives, local(): gathered = lax.all_gather(normed, ('kv', 'vocab'), axis=0, tiled=True)  48.2 us
  transfers between devices with their start and end apart: 16, of which 6 were waited for; matrix products, arithmetic and copies ran while one was open for 3% of the time, Pallas kernels for 0%

commit v1 on v0

--- a/solution.py
+++ b/solution.py
@@ -133,7 +133,10 @@
         own_state.astype(jnp.float32)
         + attention_out * row_inverse(attention_out) * norm_post_attention
     ).astype(jnp.bfloat16)
-    all_state = lax.all_gather(first_sum, ("kv", "vocab"), axis=0, tiled=True)
+    peers = lax.axis_size(("kv", "vocab"))
+    pieces = jnp.stack([first_sum for _ in range(peers)])
+    pieces = lax.all_to_all(pieces, ("kv", "vocab"), split_axis=0, concat_axis=0)
+    all_state = jnp.concatenate(pieces, axis=0)
     all_float = all_state.astype(jnp.float32)
     scaled_ffn = (all_float * norm_pre_feedforward).astype(jnp.bfloat16)
     gate_up = jnp.einsum(

time: 777 us -> 749 us (0.964)
  blocking collectives: 346 us -> 322 us
    all_gather x1 -> x0, blocking collectives: 45.5 us -> none  [local(): all_state = lax.all_gather(first_sum, ('kv', 'vocab'), axis=0, tiled=True)]
    all_to_all x0 -> x1, blocking collectives: none -> 20.5 us  [local(): lax.all_to_all(pieces, ('kv', 'vocab'), split_axis=0, concat_axis=0)]
where the time goes in v1:
time: 749 us; the launch traced here: 748 us
  waiting for transfers between devices  325 us (43%)
  blocking collectives  322 us (43%)
  starting transfers between devices  31.2 us (4%)
  matrix products  26.7 us (4%)
  between operations  16.9 us (2%)
  local copies, waits for them, and re-layouts  16.2 us (2%)
  other arithmetic  9.97 us (1%)
    unnamed x2, blocking collectives  86.2 us
    psum x1, blocking collectives, local(): totals, picked = lax.psum((totals, picked), ('kv', 'seq', 'vocab'))  76.6 us
    psum x1, waiting for transfers between devices, local(): lax.psum((numerator, jnp.sum(weights, axis=-1)), 'seq')  73.8 us
    psum x1, waiting for transfers between devices, local(): lifted = lax.psum(lifted.astype(jnp.bfloat16), 'seq').astype(jnp.float32)  64.1 us
    psum x1, waiting for transfers between devices, local(): gate_up, ffn_squares = lax.psum((gate_up, ffn_squares), 'seq')  53.8 us
    all_gather x1, waiting for transfers between devices, local(): lax.all_gather(branch, ('kv', 'vocab'), axis=2, tiled=True)  52.4 us
    psum x1, waiting for transfers between devices, local(): lax.psum((projected_rows, jnp.sum(tenant_float * tenant_float, axis=-1)),...  50.6 us
    all_gather x1, blocking collectives, local(): gathered = lax.all_gather(normed, ('kv', 'vocab'), axis=0, tiled=True)  48.2 us
  transfers between devices with their start and end apart: 16, of which 6 were waited for; matrix products, arithmetic and copies ran while one was open for 3% of the time, Pallas kernels for 0%

profile of v1, /device:TPU:1, one launch (start us, length us, event | category | flops | bytes accessed | tf_op | source)
XLA Modules:
  0.0 747.9 jit_solution(12145641892386098343)
XLA Ops:
  7.2 0.8 copy.52
  8.1 15.8 %all-gather = bf16[48,1,448]{2,1,0:T(2,128)(2,1)S(1)} all-gather(bf16[6,1,448]{2,1,0:T(2,128)(2,1)S(1)} %copy.52), channel_id=2, replica_groups=mesh['kv'=8,'seq'=8,'vocab'=4] {'kv'}, dimensions={0}, use_global_device_ids=true | all-gather | bytes 48384 | tf_op jit(solution)/shard_map/all_gather | solution.py:73
  24.0 2.2 convolution_bitcast_fusion
  26.3 15.0 %psum.85 = f32[48]{0:T(128)S(1)} all-reduce(f32[48]{0:T(128)S(1)} %fusion.56), channel_id=1, replica_groups=mesh['kv'=8,'seq'=8,'vocab'=4] {'seq'}, use_global_device_ids=true, to_apply=%region_4.5 | all-reduce | flops 48 | bytes 384 | tf_op jit(solution)/shard_map/psum | solution.py:79
  42.0 0.7 compare_bitcast_fusion
  42.7 0.8 reduce_sum.180
  43.9 50.6 %all-reduce.10.cloned.1.call-done = f32[48,1,1024]{2,0,1:T(8,128)} async-done(((f32[48,1,1024]{2,0,1:T(8,128)}), f32[48,1,1024]{2,0,1:T(8,128)}) %all-reduce.10.cloned.1.call-update) | async-done | bytes 196624 | tf_op jit(solution)/shard_map/psum | solution.py:79
  94.5 1.0 broadcast_multiply_fusion
  95.8 1.2 fusion.93
  97.1 12.7 %psum.87 = f32[48,1,2]{0,2,1:T(2,128)S(1)} all-reduce(f32[48,1,2]{0,2,1:T(2,128)S(1)} %bitcast.222), channel_id=1, replica_groups=mesh['kv'=8,'seq'=8,'vocab'=4] {'seq'}, use_global_device_ids=true, to_apply=%region_8.9 | all-reduce | flops 96 | bytes 768 | tf_op jit(solution)/shard_map/psum | solution.py:108
  109.8 1.9 convolution_bitcast_fusion.1
  112.0 73.8 %all-reduce.12.cloned.1.call-done = f32[48,1,2,256]{3,0,2,1:T(8,128)} async-done(((f32[48,1,2,256]{3,0,2,1:T(8,128)}), f32[48,1,2,256]{3,0,2,1:T(8,128)}) %all-reduce.12.cloned.1.call-update) | async-done | bytes 98320 | tf_op jit(solution)/shard_map/psum | solution.py:108
  185.8 1.1 fusion.24
  187.0 0.2 fusion.35
  187.2 18.1 %fusion = f32[8,448]{1,0:T(8,128)S(1)} fusion(f32[48,448]{1,0:T(8,128)S(1)} %fusion.35), kind=kCustom, calls=%all-reduce-scatter | all-reduce-scatter fusion | flops 28673 | bytes 101376
  205.3 3.4 collective-permute-start
  208.8 1.6 collective-permute-start.1
  210.4 0.6 dynamic-slice.6
  212.0 11.6 %psum.88 = f32[6]{0:T(128)S(1)} all-reduce(f32[6]{0:T(128)S(1)} %multiply_reduce_fusion.2), channel_id=1, replica_groups=mesh['kv'=8,'seq'=8,'vocab'=4] {'seq'}, use_global_device_ids=true, to_apply=%region_12.13 | all-reduce | flops 6 | bytes 48 | tf_op jit(solution)/shard_map/psum | solution.py:36
  223.7 20.5 %all_to_all.5 = bf16[32,6,448]{2,1,0:T(8,128)(2,1)S(1)} all-to-all(bf16[32,6,448]{2,1,0:T(8,128)(2,1)S(1)} %stack.20), channel_id=1, replica_groups=mesh['kv'=8,'seq'=8,'vocab'=4] {'kv','vocab'}, dimensions={0} | all-to-all | bytes 344064 | tf_op jit(solution)/shard_map/all_to_all | solution.py:138
  244.4 1.3 fusion.33
  246.0 11.9 %psum.90 = f32[192]{0:T(256)S(1)} all-reduce(f32[192]{0:T(256)S(1)} %reduce_sum.187), channel_id=1, replica_groups=mesh['kv'=8,'seq'=8,'vocab'=4] {'seq'}, use_global_device_ids=true, to_apply=%region_15.16 | all-reduce | flops 192 | bytes 1536 | tf_op jit(solution)/shard_map/psum | solution.py:146
  257.9 53.8 %all-reduce.14.cloned.1.call-done = f32[192,2,448]{2,0,1:T(8,128)} async-done(((f32[192,2,448]{2,0,1:T(8,128)}), f32[192,2,448]{2,0,1:T(8,128)}) %all-reduce.14.cloned.1.call-update) | async-done | bytes 688144 | tf_op jit(solution)/shard_map/psum | solution.py:146
  311.7 1.6 fusion.53
  313.3 68.1 %fusion.1 = f32[8,448]{1,0:T(8,128)S(1)} fusion(f32[192,448]{1,0:T(8,128)S(1)} %fusion.53), kind=kCustom, calls=%all-reduce-scatter.1 | all-reduce-scatter fusion | flops 114689 | bytes 359424
  381.4 1.9 collective-permute-start.2
  383.3 1.9 collective-permute-start.3
  385.2 1.4 collective-permute-start.9
  386.7 1.9 collective-permute-start.4
  388.6 1.9 collective-permute-start.5
  390.5 5.9 collective-permute-start.6
  396.4 6.8 collective-permute-start.7
  403.3 3.9 collective-permute-start.8
  407.2 0.6 dynamic-slice.10
  408.5 0.8 concatenate.35
  409.4 12.6 %psum.91 = f32[6]{0:T(128)S(1)} all-reduce(f32[6]{0:T(128)S(1)} %multiply_reduce_fusion.1), channel_id=1, replica_groups=mesh['kv'=8,'seq'=8,'vocab'=4] {'seq'}, use_global_device_ids=true, to_apply=%region_18.19 | all-reduce | flops 6 | bytes 48 | tf_op jit(solution)/shard_map/psum | solution.py:36
  422.3 10.7 %psum.92 = f32[6]{0:T(128)S(1)} all-reduce(f32[6]{0:T(128)S(1)} %get-tuple-element.17), channel_id=1, replica_groups=mesh['kv'=8,'seq'=8,'vocab'=4] {'seq'}, use_global_device_ids=true, to_apply=%region_20.21 | all-reduce | flops 6 | bytes 48 | tf_op jit(solution)/shard_map/psum | solution.py:36
  433.1 48.2 %all-gather.1 = bf16[32,6,448]{2,1,0:T(8,128)(2,1)S(1)} all-gather(bf16[1,6,448]{2,1,0:T(8,128)(2,1)S(1)} %fusion.82), channel_id=1, replica_groups=mesh['kv'=8,'seq'=8,'vocab'=4] {'kv','vocab'}, dimensions={0}, use_global_device_ids=true | all-gather | bytes 177408 | tf_op jit(solution)/shard_map/all_gather | solution.py:160
  481.4 0.9 convolution_convert_fusion.2
  482.4 0.8 reshape.415
  483.2 0.2 all-gather.6.cloned.1.call-start
  483.5 64.1 %all-reduce.16.cloned.1.call-done = bf16[192,4,112]{2,0,1:T(8,128)(2,1)} async-done(((bf16[192,4,112]{2,0,1:T(8,128)(2,1)}), bf16[192,4,112]{2,0,1:T(8,128)(2,1)}) %all-reduce.16.cloned.1.call-update) | async-done | bytes 172048 | tf_op jit(solution)/shard_map/psum | solution.py:162
  547.5 1.0 multiply_convert_fusion
  548.6 0.9 copy.60
  549.7 0.4 copy.63
  550.2 0.6 sub.35
  551.0 0.3 convert_reduce_fusion
  551.3 0.6 copy_bitcast_fusion
  551.9 0.6 copy_bitcast_fusion.2
  552.5 0.6 copy_bitcast_fusion.4
  553.1 0.6 copy_bitcast_fusion.6
  553.7 2.5 fusion.6
  556.3 1.5 fusion.8
  557.8 30.5 %all-gather.8.cloned.1.call-done = bf16[8,448,192]{1,2,0:T(8,128)(2,1)} async-done(((bf16[1,448,192]{1,2,0:T(8,128)(2,1)}), bf16[8,448,192]{1,2,0:T(8,128)(2,1)}) %all-gather.8.cloned.1.call-update) | async-done | bytes 1376272 | tf_op jit(solution)/shard_map/all_gather | solution.py:169
  588.3 2.3 copy.59
  590.6 2.7 reshape.417
  593.3 3.8 fusion.95
  597.2 52.4 %all-gather.6.cloned.1.call-done = bf16[192,4,3584]{0,1,2:T(4,128)(2,1)} async-done(((bf16[192,4,112]{0,1,2:T(4,128)(2,1)}), bf16[192,4,3584]{0,1,2:T(4,128)(2,1)}) %all-gather.6.cloned.1.call-update) | async-done | bytes 5505040 | tf_op jit(solution)/shard_map/all_gather | solution.py:177
  649.5 8.2 %fusion.17 = f32[192,4,512]{2,0,1:T(8,128)S(1)} fusion(bf16[512,3584]{1,0:T(8,128)(2,1)} %param.36, bf16[192,4,3584]{0,1,2:T(4,128)(2,1)} %all-gather.6.cloned.1.call-done, f32[192,512]{1,0:T(8,128)S(1)} %fusion.95), kind=kOutput, calls=%fused_computation.38 | convolution fusion | flops 2818965504 | bytes 11141120 | tf_op jit(solution)/shard_map/tnc,vc->tnv/dot_general | solution.py:175
  657.8 4.4 select_reduce_fusion
  662.5 0.8 reshape.406
  663.4 0.2 reshape.407
  663.6 76.6 %all-reduce.4 = (f32[192,5]{0,1:T(8,128)S(1)}, f32[5,48,4,8]{1,3,2,0:T(8,128)}) all-reduce(f32[192,5]{0,1:T(8,128)S(1)} %get-tuple-element.19, f32[5,48,4,8]{1,3,2,0:T(8,128)S(1)} %reshape.407), channel_id=1, replica_groups=mesh['kv'=8,'seq'=8,'vocab'=4] {'kv','seq','vocab'}, use_global_device_ids=true, to_apply=%region_23.24 | all-reduce | flops 8640 | bytes 69120 | tf_op jit(solution)/shard_map/psum | solution.py:203
  740.3 0.7 reshape.405
  (120 shorter events, 3.6 us)
Async XLA Ops:
  7.2 237.2 %copy-start = (bf16[448,2,448]{2,1,0:T(2,128)(2,1)S(1)}, bf16[448,2,448]{2,1,0:T(2,128)(2,1)}, u32[]{:S(2)}) copy-start(bf16[448,2,448]{2,1,0:T(2,128)(2,1)} %param.32) | copy-start | bytes 2408452
  7.2 88.7 %copy-start.2 = (bf16[1,2048,1,256]{3,1,2,0:T(8,128)(2,1)S(1)}, bf16[1,2048,1,256]{3,1,2,0:T(8,128)(2,1)}, u32[]{:S(2)}) copy-start(bf16[1,2048,1,256]{3,1,2,0:T(8,128)(2,1)} %param.27) | copy-start | bytes 3145732
  7.2 87.3 %all-reduce.10.cloned.1.call-start = ((), (), s32[]{:S(2)}) async-start(), calls=%async_computation.1 | async-start | bytes 393216 | tf_op jit(solution)/shard_map/psum | solution.py:79
  26.1 83.6 %copy-start.1 = (bf16[1,2048,1,256]{3,1,2,0:T(8,128)(2,1)S(1)}, bf16[1,2048,1,256]{3,1,2,0:T(8,128)(2,1)}, u32[]{:S(2)}) copy-start(bf16[1,2048,1,256]{3,1,2,0:T(8,128)(2,1)} %param.28) | copy-start | bytes 3145732
  26.2 159.7 %all-reduce.12.cloned.1.call-start = ((), (), s32[]{:S(2)}) async-start(), calls=%async_computation.2 | async-start | bytes 196608 | tf_op jit(solution)/shard_map/psum | solution.py:108
  97.1 89.9 %copy-start.3 = (bf16[1,512,448]{1,2,0:T(8,128)(2,1)S(1)}, bf16[1,512,448]{1,2,0:T(8,128)(2,1)}, u32[]{:S(2)}) copy-start(bf16[1,512,448]{1,2,0:T(8,128)(2,1)} %param.21) | copy-start | bytes 1376260
  97.1 113.3 %copy-start.20 = (u32[256]{0:T(256)S(1)}, u32[256]{0:T(256)}, u32[]{:S(2)}) copy-start(u32[256]{0:T(256)} %constant.87) | copy-start | bytes 3076
  97.1 126.5 %copy-start.13 = (bf16[6,1,448]{2,0,1:T(8,128)(2,1)S(1)}, bf16[6,1,448]{2,0,1:T(8,128)(2,1)}, u32[]{:S(2)}) copy-start(bf16[6,1,448]{2,0,1:T(8,128)(2,1)} %param.19) | copy-start | bytes 16132
  97.1 126.5 %copy-start.16 = (f32[448]{0:T(512)S(1)}, f32[448]{0:T(512)}, u32[]{:S(2)}) copy-start(f32[448]{0:T(512)} %param.23) | copy-start | bytes 5380
  111.7 132.6 %copy-start.14 = (f32[448]{0:T(512)S(1)}, f32[448]{0:T(512)}, u32[]{:S(2)}) copy-start(f32[448]{0:T(512)} %param.24) | copy-start | bytes 5380
  111.7 199.9 %all-reduce.14.cloned.1.call-start = ((), (), s32[]{:S(2)}) async-start(), calls=%async_computation.3 | async-start | bytes 1572864 | tf_op jit(solution)/shard_map/psum | solution.py:146
  205.3 6.3 collective-permute-start
  208.8 2.8 collective-permute-start.1
  245.6 161.6 %copy-start.19 = (u32[256]{0:T(256)S(1)}, u32[256]{0:T(256)}, u32[]{:S(2)}) copy-start(u32[256]{0:T(256)} %constant.91) | copy-start | bytes 3076
  245.6 176.5 %copy-start.17 = (f32[448]{0:T(512)S(1)}, f32[448]{0:T(512)}, u32[]{:S(2)}) copy-start(f32[448]{0:T(512)} %param.25) | copy-start | bytes 5380
  245.6 187.4 %copy-start.18 = (f32[448]{0:T(512)S(1)}, f32[448]{0:T(512)}, u32[]{:S(2)}) copy-start(f32[448]{0:T(512)} %param.26) | copy-start | bytes 5380
  245.6 235.7 %copy-start.4 = (bf16[4,448,112]{2,1,0:T(8,128)(2,1)S(1)}, bf16[4,448,112]{2,1,0:T(8,128)(2,1)}, u32[]{:S(2)}) copy-start(bf16[4,448,112]{2,1,0:T(8,128)(2,1)} %param.34) | copy-start | bytes 1204228
  245.7 301.9 %all-reduce.16.cloned.1.call-start = ((), (), s32[]{:S(2)}) async-start(), calls=%async_computation.4 | async-start | bytes 393216 | tf_op jit(solution)/shard_map/psum | solution.py:162
  313.3 234.2 %copy-start.15 = (f32[4,112]{1,0:T(4,128)S(1)}, f32[4,112]{1,0:T(4,128)}, u32[]{:S(2)}) copy-start(f32[4,112]{1,0:T(4,128)} %param.35) | copy-start | bytes 5380
  381.4 15.1 %collective-permute-start.2 = (f32[8,448]{1,0:T(8,128)S(1)}, f32[8,448]{1,0:T(8,128)S(1)}, u32[]{:S(2)}, u32[]{:S(2)}) collective-permute-start(f32[8,448]{1,0:T(8,128)S(1)} %fusion.1), channel_id=1, source_target_pairs={{0,1},{1,2},{2,3},{3,32},{32,33},{33,34},{34,35},{35,64},{64,65},{... | collective-permute-start | bytes 43016
  383.3 20.0 %collective-permute-start.3 = (f32[8,448]{1,0:T(8,128)S(1)}, f32[8,448]{1,0:T(8,128)S(1)}, u32[]{:S(2)}, u32[]{:S(2)}) collective-permute-start(f32[8,448]{1,0:T(8,128)S(1)} %fusion.1), channel_id=1, source_target_pairs={{0,2},{1,3},{2,32},{3,33},{32,34},{33,35},{34,64},{35,65},{64,66},... | collective-permute-start | bytes 43016
  385.2 164.3 %copy-start.5 = (s32[5,48,4,8]{1,3,2,0:T(8,128)S(1)}, s32[5,48,4,8]{1,3,2,0:T(8,128)}, u32[]{:S(2)}) copy-start(s32[5,48,4,8]{1,3,2,0:T(8,128)} %param.37) | copy-start | bytes 92164
  385.2 5.3 collective-permute-start.9
  386.7 21.8 %collective-permute-start.4 = (f32[8,448]{1,0:T(8,128)S(1)}, f32[8,448]{1,0:T(8,128)S(1)}, u32[]{:S(2)}, u32[]{:S(2)}) collective-permute-start(f32[8,448]{1,0:T(8,128)S(1)} %fusion.1), channel_id=1, source_target_pairs={{0,3},{1,32},{2,33},{3,34},{32,35},{33,64},{34,65},{35,66},{64,67}... | collective-permute-start | bytes 43016
  388.6 19.9 %collective-permute-start.5 = (f32[8,448]{1,0:T(8,128)S(1)}, f32[8,448]{1,0:T(8,128)S(1)}, u32[]{:S(2)}, u32[]{:S(2)}) collective-permute-start(f32[8,448]{1,0:T(8,128)S(1)} %fusion.1), channel_id=1, source_target_pairs={{0,32},{1,33},{2,34},{3,35},{32,64},{33,65},{34,66},{35,67},{64,96... | collective-permute-start | bytes 43016
  390.5 17.9 %collective-permute-start.6 = (f32[8,448]{1,0:T(8,128)S(1)}, f32[8,448]{1,0:T(8,128)S(1)}, u32[]{:S(2)}, u32[]{:S(2)}) collective-permute-start(f32[8,448]{1,0:T(8,128)S(1)} %fusion.1), channel_id=1, source_target_pairs={{0,33},{1,34},{2,35},{3,64},{32,65},{33,66},{34,67},{35,96},{64,97... | collective-permute-start | bytes 43016
  396.4 12.1 %collective-permute-start.7 = (f32[8,448]{1,0:T(8,128)S(1)}, f32[8,448]{1,0:T(8,128)S(1)}, u32[]{:S(2)}, u32[]{:S(2)}) collective-permute-start(f32[8,448]{1,0:T(8,128)S(1)} %fusion.1), channel_id=1, source_target_pairs={{0,34},{1,35},{2,64},{3,65},{32,66},{33,67},{34,96},{35,97},{64,98... | collective-permute-start | bytes 43016
  403.3 5.2 collective-permute-start.8
  482.3 106.0 %all-gather.8.cloned.1.call-start = ((), (), s32[]{:S(2)}) async-start(), calls=%async_computation.6 | async-start | bytes 1769472 | tf_op jit(solution)/shard_map/all_gather | solution.py:169
  483.2 67.6 %copy-start.21 = (s32[1,5]{1,0:T(1,128)S(1)}, s32[1,5]{1,0:T(1,128)}, u32[]{:S(2)}) copy-start(s32[1,5]{1,0:T(1,128)} %param.31) | copy-start | bytes 64
  483.2 166.3 %all-gather.6.cloned.1.call-start = ((), (), s32[]{:S(2)}) async-start(), calls=%async_computation.5 | async-start | bytes 7569408 | tf_op jit(solution)/shard_map/all_gather | solution.py:177
  597.1 60.7 %copy-start.6 = (s32[192,5]{0,1:T(8,128)S(1)}, s32[192,5]{0,1:T(8,128)}, u32[]{:S(2)}) copy-start(s32[192,5]{0,1:T(8,128)} %get-tuple-element.43) | copy-start | bytes 11524
  597.1 60.7 %copy-start.7 = (s32[192,5]{0,1:T(8,128)S(1)}, s32[192,5]{0,1:T(8,128)}, u32[]{:S(2)}) copy-start(s32[192,5]{0,1:T(8,128)} %get-tuple-element.44) | copy-start | bytes 11524
  597.1 60.7 %copy-start.8 = (s32[192,5]{0,1:T(8,128)S(1)}, s32[192,5]{0,1:T(8,128)}, u32[]{:S(2)}) copy-start(s32[192,5]{0,1:T(8,128)} %get-tuple-element.45) | copy-start | bytes 11524
  597.1 60.7 %copy-start.9 = (s32[192,5]{0,1:T(8,128)S(1)}, s32[192,5]{0,1:T(8,128)}, u32[]{:S(2)}) copy-start(s32[192,5]{0,1:T(8,128)} %get-tuple-element.46) | copy-start | bytes 11524
  597.2 60.7 %copy-start.10 = (s32[192,5]{0,1:T(8,128)S(1)}, s32[192,5]{0,1:T(8,128)}, u32[]{:S(2)}) copy-start(s32[192,5]{0,1:T(8,128)} %get-tuple-element.47) | copy-start | bytes 11524
  597.2 60.7 %copy-start.11 = (s32[192,5]{0,1:T(8,128)S(1)}, s32[192,5]{0,1:T(8,128)}, u32[]{:S(2)}) copy-start(s32[192,5]{0,1:T(8,128)} %get-tuple-element.48) | copy-start | bytes 11524
  597.2 60.7 %copy-start.12 = (s32[192,5]{0,1:T(8,128)S(1)}, s32[192,5]{0,1:T(8,128)}, u32[]{:S(2)}) copy-start(s32[192,5]{0,1:T(8,128)} %get-tuple-element.49) | copy-start | bytes 11524
Sparse Core Ops, SparseCore 0:
  26.3 68.1 all-reduce.9
  111.9 73.9 all-reduce.11
  245.8 65.8 all-reduce.13
  482.5 65.0 all-reduce.15
  549.2 39.1 all-gather.7
  590.8 58.7 all-gather.5
